TPU v7x, 32 devices: a whole 2x2x4 slice. The times are simulated.
32 devices in a mesh: replica: 4 (over y, x), fsdp: 8 (over z, core).
Axes of the slice: x: 2, y: 2, z: 4, core: 2. Of those that a mesh axis runs over, the one named last changes fastest.
Arguments:
- hidden_in: bfloat16 [8192, 1024], P(('replica', 'fsdp')), may hold values from -8 to 8
- seq_lengths: int32 [32, 4], P(('replica', 'fsdp')), may hold values from 0 to 256, as said below
- routes: int32 [8192, 8], P(('replica', 'fsdp')), may hold values from 0 to 15, all different within a row; in each aligned block of 256 rows (0 to 255, 256 to 511, ...) at most 144 rows name the same one
- norm1_gain: bfloat16 [1024], P('fsdp'), may hold values from 0.25 to 1.75
- w_query: bfloat16 [1024, 1024], P('fsdp'), may hold values from -1 to 1
- w_key: bfloat16 [1024, 512], P('fsdp'), may hold values from -1 to 1
- w_value: bfloat16 [1024, 512], P('fsdp'), may hold values from -0.1875 to 0.1875
- w_output: bfloat16 [1024, 1024], P('fsdp'), may hold values from -6 to 6
- norm2_gain: bfloat16 [1024], P('fsdp'), may hold values from 0.25 to 1.75
- w_router: bfloat16 [1024, 16], P('fsdp'), may hold values from -3 to 3
- expert_weights: bfloat16 [16, 1536, 1024], P('fsdp'), may hold values from -3 to 3
- out_cotangent: bfloat16 [8192, 1024], P(('replica', 'fsdp')), may hold values from -6 to 6
Outputs:
- layer_out: bfloat16 [8192, 1024], P(('replica', 'fsdp'))
- grad_in: float32 [8192, 1024], P(('replica', 'fsdp'))
- grad_norm1: float32 [1024], P('fsdp')
- grad_query: float32 [1024, 1024], P('fsdp')
- grad_key: float32 [1024, 512], P('fsdp')
- grad_value: float32 [1024, 512], P('fsdp')
- grad_output: float32 [1024, 1024], P('fsdp')
- grad_norm2: float32 [1024], P('fsdp')
- grad_router: float32 [1024, 16], P('fsdp')
- grad_experts: float32 [16, 1536, 1024], P('fsdp')
Inputs may be any that keep to these rules, and one draw needn't show every extreme that they name: `seq_lengths`: each row sums to 256; a length may be 0; some row holds one sequence of 256. `routes`: A token's experts differ; among the rows of one device no expert is named more than 144 times, a bound that some block reaches.
All inputs are finite; a program needn't handle non-finite values.
Results may differ from a plain program's by a relative error of at most 0.015.
The roundings to bfloat16 on the way count: a program that leaves them out, or rounds other values in their place, can miss the bound.
Values may be sent and summed in bfloat16 or wider, within the bound.
A program may use at most 384 MiB of HBM per device.

v0:
```python
import jax
import jax.numpy as jnp
from jax import lax
from jax.sharding import PartitionSpec as P

D = 1024
H = 16
KVH = 8
HD = 64
FF = 512
TOPK = 8
E = 16
CAP = 144
norm_eps = 1e-06
score_scale = 0.015625
residual_scale = 0.22
rope_base = 10000.0
masked_score = -1e30


def inverse_rms(vector):
    return lax.rsqrt(jnp.mean(vector * vector, axis=-1, keepdims=True) + norm_eps)


def rms_back(vector, factor, gain_full, incoming):
    scaled = incoming * gain_full
    grad_gain = jnp.sum(incoming * vector * factor, axis=0)
    grad_vector = factor * scaled - vector * factor**3 * jnp.mean(
        scaled * vector, axis=-1, keepdims=True
    )
    return (grad_vector, grad_gain)


def rotate(vector, cosines, sine_table):
    half_size = vector.shape[-1] // 2
    turned = jnp.concatenate([-vector[..., half_size:], vector[..., :half_size]], axis=-1)
    return vector * cosines[:, None, :] + turned * sine_table[:, None, :]


def expert_forward(slot_inputs, weight_rows):
    gate_pre = jnp.einsum(
        "ecd,efd->ecf", slot_inputs, weight_rows[:, :FF], preferred_element_type=jnp.float32
    )
    up_pre = jnp.einsum(
        "ecd,efd->ecf", slot_inputs, weight_rows[:, FF : 2 * FF], preferred_element_type=jnp.float32
    )
    hidden_act = (jax.nn.silu(gate_pre) * up_pre).astype(jnp.bfloat16)
    produced = jnp.einsum(
        "ecf,efd->ecd", hidden_act, weight_rows[:, 2 * FF :], preferred_element_type=jnp.float32
    )
    return (produced.astype(jnp.bfloat16), gate_pre, up_pre)


def expert_backward(slot_grads, gate_pre, up_pre, weight_rows):
    sigmoid_gate = jax.nn.sigmoid(gate_pre)
    grad_act = jnp.einsum(
        "ecd,efd->ecf", slot_grads, weight_rows[:, 2 * FF :], preferred_element_type=jnp.float32
    )
    grad_gate = (
        grad_act * up_pre * (sigmoid_gate * (1.0 + gate_pre * (1.0 - sigmoid_gate)))
    ).astype(jnp.bfloat16)
    grad_up = (grad_act * jax.nn.silu(gate_pre)).astype(jnp.bfloat16)
    grad_rows = jnp.einsum(
        "ecf,efd->ecd", grad_gate, weight_rows[:, :FF], preferred_element_type=jnp.float32
    )
    grad_rows = grad_rows + jnp.einsum(
        "ecf,efd->ecd", grad_up, weight_rows[:, FF : 2 * FF], preferred_element_type=jnp.float32
    )
    return (grad_gate, grad_up, grad_rows.astype(jnp.bfloat16))


def expert_grads(slot_inputs, slot_grads, gate_pre, up_pre, grad_gate, grad_up):
    hidden_act = (jax.nn.silu(gate_pre) * up_pre).astype(jnp.bfloat16)
    return jnp.concatenate(
        [
            jnp.einsum("ecf,ecd->efd", grad_gate, slot_inputs, preferred_element_type=jnp.float32),
            jnp.einsum("ecf,ecd->efd", grad_up, slot_inputs, preferred_element_type=jnp.float32),
            jnp.einsum("ecf,ecd->efd", hidden_act, slot_grads, preferred_element_type=jnp.float32),
        ],
        axis=1,
    )


def body(
    hidden_in,
    seq_lengths,
    routes,
    norm1_gain,
    w_query,
    w_key,
    w_value,
    w_output,
    norm2_gain,
    w_router,
    expert_weights,
    out_cotangent,
):
    gain_one, query_w, key_w, value_w, output_w, gain_two, router_w = (
        lax.all_gather(norm1_gain, "fsdp", axis=0, tiled=True),
        lax.all_gather(w_query, "fsdp", axis=0, tiled=True),
        lax.all_gather(w_key, "fsdp", axis=0, tiled=True),
        lax.all_gather(w_value, "fsdp", axis=0, tiled=True),
        lax.all_gather(w_output, "fsdp", axis=0, tiled=True),
        lax.all_gather(norm2_gain, "fsdp", axis=0, tiled=True),
        lax.all_gather(w_router, "fsdp", axis=0, tiled=True),
    )
    tokens = hidden_in.shape[0]
    group = H // KVH
    block_rows = min(512, tokens)
    token_index = jnp.arange(tokens, dtype=jnp.int32)
    seq_ends = jnp.cumsum(seq_lengths[0])
    passed = token_index[:, None] >= seq_ends[None, :]
    segment = jnp.sum(passed.astype(jnp.int32), axis=1)
    position = token_index - jnp.max(jnp.where(passed, seq_ends[None, :], 0), axis=1)
    frequency = rope_base ** (-jnp.arange(0, HD, 2, dtype=jnp.float32) / HD)
    angles = position.astype(jnp.float32)[:, None] * frequency[None, :]
    angles = jnp.concatenate([angles, angles], axis=1)
    cosines = jnp.cos(angles)
    sine_table = jnp.sin(angles)
    allowed = (segment[:, None] == segment[None, :]) & (
        token_index[None, :] <= token_index[:, None]
    )
    source = hidden_in.astype(jnp.float32)
    factor_one = inverse_rms(source)
    gain_first = gain_one.astype(jnp.float32)
    normed = (source * factor_one * gain_first).astype(jnp.bfloat16)
    query_rot = rotate(
        jnp.dot(normed, query_w, preferred_element_type=jnp.float32).reshape(tokens, H, HD),
        cosines,
        sine_table,
    )
    query_rot = query_rot.astype(jnp.bfloat16).reshape(tokens, KVH, group, HD)
    key_rot = rotate(
        jnp.dot(normed, key_w, preferred_element_type=jnp.float32).reshape(tokens, KVH, HD),
        cosines,
        sine_table,
    )
    key_rot = key_rot.astype(jnp.bfloat16)
    value_rows = (
        jnp.dot(normed, value_w, preferred_element_type=jnp.float32)
        .astype(jnp.bfloat16)
        .reshape(tokens, KVH, HD)
    )

    def block_scores():
        raw_scores = (
            jnp.einsum("qkgd,tkd->kgqt", query_rot, key_rot, preferred_element_type=jnp.float32)
            * score_scale
        )
        return jnp.where(allowed[None, None], raw_scores, masked_score)

    scores = block_scores()
    row_max = jnp.max(scores, axis=-1, keepdims=True)
    shifted = jnp.exp(scores - row_max)
    row_total = jnp.sum(shifted, axis=-1, keepdims=True)
    weights = (shifted / row_total).astype(jnp.bfloat16)
    mixed_parts = jnp.einsum(
        "kgqt,tkd->qkgd", weights, value_rows, preferred_element_type=jnp.float32
    )
    log_totals = [row_max + jnp.log(row_total)]
    mixed = mixed_parts.reshape(tokens, H * HD).astype(jnp.bfloat16)
    after = source + residual_scale * jnp.dot(mixed, output_w, preferred_element_type=jnp.float32)
    factor_two = inverse_rms(after)
    gain_second = gain_two.astype(jnp.float32)
    normed_two = (after * factor_two * gain_second).astype(jnp.bfloat16)
    logits = jnp.dot(normed_two, router_w, preferred_element_type=jnp.float32)
    route_hits = (routes[:, :, None] == jnp.arange(E, dtype=jnp.int32)[None, None, :]).astype(
        jnp.float32
    )
    chosen = jnp.sum(route_hits * logits[:, None, :], axis=2)
    gate_probs = jax.nn.softmax(chosen, axis=1)
    flat_routes = routes.reshape(-1)
    flat_hits = (flat_routes[:, None] == jnp.arange(E, dtype=jnp.int32)[None, :]).astype(jnp.int32)
    slot_rank = jnp.sum((jnp.cumsum(flat_hits, axis=0) - flat_hits) * flat_hits, axis=1)
    slot_ids = flat_routes * CAP + slot_rank
    numbered = jnp.arange(tokens * TOPK, dtype=jnp.int32) + 1
    slot_owner = jnp.zeros((E * CAP,), jnp.int32).at[slot_ids].set(numbered) - 1
    filled = slot_owner >= 0
    owner_rows = jnp.maximum(slot_owner, 0)
    zero_half = jnp.zeros((), jnp.bfloat16)
    slot_inputs = jnp.where(filled[:, None], normed_two[owner_rows // TOPK], zero_half).reshape(
        E, CAP, D
    )
    produced, gate_pre, up_pre = expert_forward(
        slot_inputs, lax.all_gather(expert_weights, "fsdp", axis=0, tiled=True)
    )
    picked = produced.reshape(E * CAP, D)[slot_ids].reshape(tokens, TOPK, D)
    mixture = jnp.einsum("tk,tkd->td", gate_probs, picked, preferred_element_type=jnp.float32)
    layer_out = (after + residual_scale * mixture).astype(jnp.bfloat16)
    grad_out = out_cotangent.astype(jnp.float32)
    grad_moe = residual_scale * grad_out
    grad_gates = jnp.einsum("td,tkd->tk", grad_moe, picked, preferred_element_type=jnp.float32)
    grad_chosen = gate_probs * (
        grad_gates - jnp.sum(gate_probs * grad_gates, axis=1, keepdims=True)
    )
    grad_logits = jnp.sum(route_hits * grad_chosen[:, :, None], axis=1).astype(jnp.bfloat16)
    grad_router = jnp.einsum(
        "td,te->de", normed_two, grad_logits, preferred_element_type=jnp.float32
    )
    grad_picked = (
        (gate_probs[:, :, None] * grad_moe[:, None, :])
        .astype(jnp.bfloat16)
        .reshape(tokens * TOPK, D)
    )
    slot_grads = jnp.where(filled[:, None], grad_picked[owner_rows], zero_half).reshape(E, CAP, D)
    grad_gate, grad_up, grad_rows = expert_backward(
        slot_grads, gate_pre, up_pre, lax.all_gather(expert_weights, "fsdp", axis=0, tiled=True)
    )
    grad_expert_shard = lax.psum_scatter(
        expert_grads(slot_inputs, slot_grads, gate_pre, up_pre, grad_gate, grad_up),
        "fsdp",
        scatter_dimension=0,
        tiled=True,
    )
    returned = grad_rows.reshape(E * CAP, D)[slot_ids].reshape(tokens, TOPK, D)
    grad_normed_two = jnp.einsum(
        "te,de->td", grad_logits, router_w, preferred_element_type=jnp.float32
    )
    grad_normed_two = grad_normed_two + jnp.sum(returned, axis=1, dtype=jnp.float32)
    grad_after_norm, grad_gain_two = rms_back(after, factor_two, gain_second, grad_normed_two)
    grad_after = grad_out + grad_after_norm
    grad_branch = (residual_scale * grad_after).astype(jnp.bfloat16)
    grad_output_w = jnp.einsum("tc,td->cd", mixed, grad_branch, preferred_element_type=jnp.float32)
    grad_mixed = jnp.einsum("td,cd->tc", grad_branch, output_w, preferred_element_type=jnp.float32)
    grad_mixed = grad_mixed.astype(jnp.bfloat16).reshape(tokens, KVH, group, HD)
    query_parts = []
    grad_key_rot = jnp.zeros((tokens, KVH, HD), jnp.float32)
    grad_value_rows = jnp.zeros((tokens, KVH, HD), jnp.float32)
    for number, offset in enumerate(range(0, tokens, block_rows)):
        scores = block_scores()
        weights_full = jnp.exp(scores - log_totals[number])
        grad_weights = jnp.einsum(
            "qkgd,tkd->kgqt", grad_mixed, value_rows, preferred_element_type=jnp.float32
        )
        grad_scores = weights_full * (
            grad_weights - jnp.sum(weights_full * grad_weights, axis=-1, keepdims=True)
        )
        grad_scores = grad_scores.astype(jnp.bfloat16)
        query_parts.append(
            jnp.einsum("kgqt,tkd->qkgd", grad_scores, key_rot, preferred_element_type=jnp.float32)
            * score_scale
        )
        grad_key_rot = (
            jnp.einsum("kgqt,qkgd->tkd", grad_scores, query_rot, preferred_element_type=jnp.float32)
            * score_scale
        )
        grad_value_rows = jnp.einsum(
            "kgqt,qkgd->tkd",
            weights_full.astype(jnp.bfloat16),
            grad_mixed,
            preferred_element_type=jnp.float32,
        )
    grad_query_rows = rotate(query_parts[0].reshape(tokens, H, HD), cosines, -sine_table)
    grad_query_rows = grad_query_rows.astype(jnp.bfloat16).reshape(tokens, H * HD)
    grad_key_rows = (
        rotate(grad_key_rot, cosines, -sine_table).astype(jnp.bfloat16).reshape(tokens, KVH * HD)
    )
    grad_value_flat = grad_value_rows.astype(jnp.bfloat16).reshape(tokens, KVH * HD)
    grad_query_w = jnp.einsum(
        "td,tc->dc", normed, grad_query_rows, preferred_element_type=jnp.float32
    )
    grad_key_w = jnp.einsum("td,tc->dc", normed, grad_key_rows, preferred_element_type=jnp.float32)
    grad_value_w = jnp.einsum(
        "td,tc->dc", normed, grad_value_flat, preferred_element_type=jnp.float32
    )
    grad_normed = jnp.einsum(
        "tc,dc->td", grad_query_rows, query_w, preferred_element_type=jnp.float32
    )
    grad_normed = grad_normed + jnp.einsum(
        "tc,dc->td", grad_key_rows, key_w, preferred_element_type=jnp.float32
    )
    grad_normed = grad_normed + jnp.einsum(
        "tc,dc->td", grad_value_flat, value_w, preferred_element_type=jnp.float32
    )
    grad_input_norm, grad_gain_one = rms_back(source, factor_one, gain_first, grad_normed)
    grad_in = grad_after + grad_input_norm
    (
        shard_gain_one,
        shard_query,
        shard_key,
        shard_value,
        shard_output,
        shard_gain_two,
        shard_router,
    ) = (
        lax.psum_scatter(grad_gain_one, "fsdp", scatter_dimension=0, tiled=True),
        lax.psum_scatter(grad_query_w, "fsdp", scatter_dimension=0, tiled=True),
        lax.psum_scatter(grad_key_w, "fsdp", scatter_dimension=0, tiled=True),
        lax.psum_scatter(grad_value_w, "fsdp", scatter_dimension=0, tiled=True),
        lax.psum_scatter(grad_output_w, "fsdp", scatter_dimension=0, tiled=True),
        lax.psum_scatter(grad_gain_two, "fsdp", scatter_dimension=0, tiled=True),
        lax.psum_scatter(grad_router, "fsdp", scatter_dimension=0, tiled=True),
    )
    summed = lax.psum(
        (
            shard_gain_one,
            shard_query,
            shard_key,
            shard_value,
            shard_output,
            shard_gain_two,
            shard_router,
            grad_expert_shard,
        ),
        "replica",
    )
    return (
        layer_out,
        grad_in,
        summed[0],
        summed[1],
        summed[2],
        summed[3],
        summed[4],
        summed[5],
        summed[6],
        summed[7],
    )


def solution(mesh):
    return jax.shard_map(
        body,
        mesh=mesh,
        in_specs=(
            P(("replica", "fsdp"), None),
            P(("replica", "fsdp"), None),
            P(("replica", "fsdp"), None),
            P("fsdp"),
            P("fsdp", None),
            P("fsdp", None),
            P("fsdp", None),
            P("fsdp", None),
            P("fsdp"),
            P("fsdp", None),
            P("fsdp", None, None),
            P(("replica", "fsdp"), None),
        ),
        out_specs=(
            P(("replica", "fsdp"), None),
            P(("replica", "fsdp"), None),
            P("fsdp"),
            P("fsdp", None),
            P("fsdp", None),
            P("fsdp", None),
            P("fsdp", None),
            P("fsdp"),
            P("fsdp", None),
            P("fsdp", None, None),
        ),
        check_vma=False,
    )
```

profile of v0, /device:TPU:0, one launch (start us, length us, event | category | flops | bytes accessed | tf_op | source)
XLA Modules:
  0.0 2149.8 jit_solution(16897767280440720643)
XLA Ops:
  11.1 13.5 all-gather
  47.2 12.7 all_gather.31
  66.9 21.5 all-gather.12.cloned.1.call-done
  95.8 22.7 %all-gather.14.cloned.1.call-done = bf16[1024,1024]{1,0:T(8,128)(2,1)} async-done(((bf16[128,1024]{1,0:T(8,128)(2,1)}), bf16[1024,1024]{1,0:T(8,128)(2,1)}) %all-gather.14.cloned.1.call-update) | async-done | bytes 2097168 | tf_op jit(solution)/shard_map/all_gather | solution.py:103
  131.3 415.6 %all-gather.16.cloned.1.call-done = bf16[16,1536,1024]{2,1,0:T(8,128)(2,1)} async-done(((bf16[2,1536,1024]{2,1,0:T(8,128)(2,1)}), bf16[16,1536,1024]{2,1,0:T(8,128)(2,1)}) %all-gather.16.cloned.1.call-update) | async-done | bytes 50331664 | tf_op jit(solution)/shard_map/all_gather | solution.py:185
  546.9 11.5 fusion.10
  558.4 13.0 multiply_convert_fusion.2
  571.4 11.4 fusion.26
  582.8 14.4 gather_fusion.1
  609.1 13.7 gather_fusion.2
  622.8 14.3 multiply_convert_fusion.1
  637.1 12.3 fusion.4
  649.4 12.3 add_convert_fusion
  661.7 13.9 gather_fusion.3
  713.1 19.0 fusion.21
  732.5 19.3 fusion.25
  751.8 18.2 fusion.24
  770.0 67.1 %pad_maximum_fusion = f32[16,1536,1024]{2,1,0:T(8,128)} fusion(f32[16,512,1024]{2,1,0:T(8,128)} %fusion.21, f32[16,512,1024]{2,1,0:T(8,128)} %fusion.24, f32[16,512,1024]{2,1,0:T(8,128)} %fusion.25), kind=kLoop, calls=%fused_computation.5 | loop fusion | flops 50331648 | bytes 201326592 | tf_op jit(solution)/shard_map/concatenate | solution.py:74
  839.1 27.1 %reduce-scatter.7.cloned.1.call-done = f32[128,1024]{1,0:T(8,128)} async-done(((f32[1024,1024]{1,0:T(8,128)}), f32[128,1024]{1,0:T(8,128)}) %reduce-scatter.7.cloned.1.call-update) | async-done | bytes 524304 | tf_op jit(solution)/shard_map/reduce_scatter | solution.py:287
  866.2 955.4 %reduce-scatter.17.cloned.1.call-done = f32[2,1536,1024]{2,1,0:T(8,128)} async-done(((f32[16,1536,1024]{2,1,0:T(8,128)}), f32[2,1536,1024]{2,1,0:T(8,128)}) %reduce-scatter.17.cloned.1.call-update) | async-done | bytes 12582928 | tf_op jit(solution)/shard_map/reduce_scatter | solution.py:209
  1829.7 13.9 all-reduce.2
  1852.9 11.0 all-reduce.3
  1863.9 259.5 %all-reduce.7.cloned.1.call-done = (f32[128,1024]{1,0:T(8,128)}, f32[128,512]{1,0:T(8,128)}, f32[128,512]{1,0:T(8,128)}, f32[128,1024]{1,0:T(8,128)}, f32[2,1536,1024]{2,1,0:T(8,128)}) async-done(((f32[128,1024]{1,0:T(8,128)}, f32[128,512]{1,0:T(8,128)}, f32[128,512]{1,0:T(8,128)}, f32[128,1024]{1,0:T(8,128)}, f32[2,1536,1024]{2,1,0:T(8,128)}), (f32[128,1024]{1,0:T(8,128)}, f32[128,512]{1,0:T(8,128)}, ...) | async-done | bytes 14155792 | tf_op jit(solution)/shard_map/psum | solution.py:294
  2130.5 12.1 copy.107
  (245 shorter events, 128.3 us)
Async XLA Ops:
  7.2 26.3 %copy-start.57 = (s32[1,4]{1,0:T(1,128)S(1)}, s32[1,4]{1,0:T(1,128)}, u32[]{:S(2)}) copy-start(s32[1,4]{1,0:T(1,128)} %param.13) | copy-start | bytes 52
  7.2 40.0 %copy-start.54 = (bf16[128,16]{0,1:T(8,128)(2,1)S(1)}, bf16[128,16]{0,1:T(8,128)(2,1)}, u32[]{:S(2)}) copy-start(bf16[128,16]{0,1:T(8,128)(2,1)} %param.21) | copy-start | bytes 12292
  7.2 53.7 %copy-start.4 = (bf16[256,1024]{1,0:T(8,128)(2,1)S(1)}, bf16[256,1024]{1,0:T(8,128)(2,1)}, u32[]{:S(2)}) copy-start(bf16[256,1024]{1,0:T(8,128)(2,1)} %param.12) | copy-start | bytes 1572868
  7.2 55.7 %all-gather.8.cloned.1.call-start = ((), (), s32[]{:S(2)}) async-start(), calls=%async_computation.6 | async-start | bytes 1179648 | tf_op jit(solution)/shard_map/all_gather | solution.py:102
  8.0 56.8 %all-gather.10.cloned.1.call-start = ((), (), s32[]{:S(2)}) async-start(), calls=%async_computation.7 | async-start | bytes 1179648 | tf_op jit(solution)/shard_map/all_gather | solution.py:101
  8.7 79.7 %all-gather.12.cloned.1.call-start = ((), (), s32[]{:S(2)}) async-start(), calls=%async_computation.8 | async-start | bytes 2359296 | tf_op jit(solution)/shard_map/all_gather | solution.py:100
  9.5 52.4 %copy-start.15 = (bf16[256,1024]{1,0:T(8,128)(2,1)S(1)}, bf16[256,1024]{1,0:T(8,128)(2,1)}, u32[]{:S(2)}) copy-start(bf16[256,1024]{1,0:T(8,128)(2,1)} %param.23) | copy-start | bytes 1572868
  9.5 109.0 %all-gather.14.cloned.1.call-start = ((), (), s32[]{:S(2)}) async-start(), calls=%async_computation.9 | async-start | bytes 2359296 | tf_op jit(solution)/shard_map/all_gather | solution.py:103
  10.0 536.9 %all-gather.16.cloned.1.call-start = ((), (), s32[]{:S(2)}) async-start(), calls=%async_computation.10 | async-start | bytes 56623104 | tf_op jit(solution)/shard_map/all_gather | solution.py:185
  10.6 828.4 %reduce-scatter.11.cloned.1.call-start = ((), (), s32[]{:S(2)}) async-start(), calls=%async_computation.13 | async-start | bytes 2359296 | tf_op jit(solution)/shard_map/reduce_scatter | solution.py:289
  24.5 63.9 %copy-start.38 = (f32[8,1,128]{2,1,0:T(1,128)}, f32[8,1,128]{2,1,0:T(1,128)S(1)}, u32[]{:S(2)}) copy-start(f32[8,1,128]{2,1,0:T(1,128)S(1)} %convert_element_type.151) | copy-start | bytes 12292
  33.2 88.4 %copy-start.44 = (f32[8,1,128]{2,1,0:T(1,128)}, f32[8,1,128]{2,1,0:T(1,128)S(1)}, u32[]{:S(2)}) copy-start(f32[8,1,128]{2,1,0:T(1,128)S(1)} %convert_element_type.152) | copy-start | bytes 12292
  59.9 70.4 %copy-start.34 = (bf16[1024,16]{0,1:T(8,128)(2,1)}, bf16[1024,16]{0,1:T(8,128)(2,1)S(1)}, u32[]{:S(2)}) copy-start(bf16[1024,16]{0,1:T(8,128)(2,1)S(1)} %all_gather.31) | copy-start | bytes 98308
  61.0 30.1 %copy-start.30 = (f32[256,64]{0,1:T(8,128)}, f32[256,64]{0,1:T(8,128)S(1)}, u32[]{:S(2)}) copy-start(f32[256,64]{0,1:T(8,128)S(1)} %get-tuple-element.43) | copy-start | bytes 196612
  61.8 26.6 %copy-start.46 = (f32[256]{0:T(256)}, f32[256]{0:T(256)S(1)}, u32[]{:S(2)}) copy-start(f32[256]{0:T(256)S(1)} %get-tuple-element.47) | copy-start | bytes 3076
  64.8 28.8 %copy-start.29 = (bf16[256,512]{0,1:T(8,128)(2,1)}, bf16[256,512]{0,1:T(8,128)(2,1)S(1)}, u32[]{:S(2)}) copy-start(bf16[256,512]{0,1:T(8,128)(2,1)S(1)} %copy.66) | copy-start | bytes 786436
  95.8 34.6 %copy-start.28 = (bf16[8,64,2,256]{3,1,2,0:T(8,128)(2,1)}, bf16[8,64,2,256]{3,1,2,0:T(8,128)(2,1)S(1)}, u32[]{:S(2)}) copy-start(bf16[8,64,2,256]{3,1,2,0:T(8,128)(2,1)S(1)} %fusion.41) | copy-start | bytes 1572868
  602.0 79.2 %copy-start.42 = (bf16[256,16]{0,1:T(8,128)(2,1)}, bf16[256,16]{0,1:T(8,128)(2,1)S(1)}, u32[]{:S(2)}) copy-start(bf16[256,16]{0,1:T(8,128)(2,1)S(1)} %select_reduce_fusion) | copy-start | bytes 24580
  693.2 145.9 %reduce-scatter.9.cloned.1.call-start = ((), (), s32[]{:S(2)}) async-start(), calls=%async_computation.12 | async-start | bytes 2359296 | tf_op jit(solution)/shard_map/reduce_scatter | solution.py:288
  702.7 136.4 %reduce-scatter.13.cloned.1.call-start = ((), (), s32[]{:S(2)}) async-start(), calls=%async_computation.14 | async-start | bytes 4718592 | tf_op jit(solution)/shard_map/reduce_scatter | solution.py:290
  706.9 159.3 %reduce-scatter.7.cloned.1.call-start = ((), (), s32[]{:S(2)}) async-start(), calls=%async_computation.11 | async-start | bytes 4718592 | tf_op jit(solution)/shard_map/reduce_scatter | solution.py:287
  732.2 1089.4 %reduce-scatter.17.cloned.1.call-start = ((), (), s32[]{:S(2)}) async-start(), calls=%async_computation.16 | async-start | bytes 113246208 | tf_op jit(solution)/shard_map/reduce_scatter | solution.py:209
  837.2 1015.8 %reduce-scatter.15.cloned.1.call-start = ((), (), s32[]{:S(2)}) async-start(), calls=%async_computation.15 | async-start | bytes 73728 | tf_op jit(solution)/shard_map/reduce_scatter | solution.py:292
  839.0 1284.4 %all-reduce.7.cloned.1.call-start = ((), (), s32[]{:S(2)}) async-start(), calls=%async_computation.17 | async-start | bytes 28311552 | tf_op jit(solution)/shard_map/psum | solution.py:294
  (47 other events, 279.8 us)
Sparse Core Ops, SparseCore 0:
  9.7 24.7 all-gather.7
  36.1 21.8 all-gather.9
  59.6 28.7 all-gather.11
  89.9 28.5 all-gather.13
  120.0 426.8 all-gather.15
  693.3 33.9 reduce-scatter.10
  729.6 34.5 reduce-scatter.8
  766.5 48.5 reduce-scatter.12
  818.0 48.1 reduce-scatter.6
  868.4 953.1 reduce-scatter.16
  1824.5 28.3 reduce-scatter.14
  1857.1 266.2 all-reduce.6
where the time goes:
time: 2160 us; the launch traced here: 2150 us
  waiting for transfers between devices  1710 us (79%)
  matrix products  181 us (8%)
  local copies, waits for them, and re-layouts  90.1 us (4%)
  other arithmetic  89.7 us (4%)
  blocking collectives  59.8 us (3%)
    reduce_scatter x1, waiting for transfers between devices, body(): lax.psum_scatter(expert_grads(slot_inputs, slot_grads, gate_pre, up_pre,...  955 us
    all_gather x1, waiting for transfers between devices, body(): lax.all_gather(expert_weights, 'fsdp', axis=0, tiled=True)  416 us
    psum x1, waiting for transfers between devices, body(): lax.psum((shard_gain_one, shard_query, shard_key, shard_value, shard_outp...  259 us
    concatenate x1, other arithmetic, expert_grads(): jnp.concatenate([jnp.einsum('ecf,ecd->efd', grad_gate, slot_inputs, prefe...  67.1 us
  transfers between devices with their start and end apart: 12, of which 7 were waited for; matrix products, arithmetic and copies ran while one was open for 9% of the time, Pallas kernels for 0%

commit v1 on v0

--- a/solution.py
+++ b/solution.py
@@ -16,6 +16,28 @@
 residual_scale = 0.22
 rope_base = 10000.0
 masked_score = -1e30
+
+
+def joined_along(pieces, dim):
+    dims = list(pieces.shape[1:])
+    dims[dim] *= pieces.shape[0]
+    return jnp.moveaxis(pieces, 0, dim).reshape(dims)
+
+
+def ring_gather(x, axis, dim):
+    peers = lax.axis_size(axis)
+    pairs = [(i, (i + 1) % peers) for i in range(peers)]
+    back = [(b, a) for a, b in pairs]
+    lower, upper = ([], [])
+    for turn in range(peers - 1):
+        if turn % 2 == 0:
+            lower.append(lax.ppermute(lower[-1] if lower else x, axis, pairs))
+        else:
+            upper.append(lax.ppermute(upper[-1] if upper else x, axis, back))
+    tiles = jnp.stack([*lower[::-1], x, *upper])
+    shift = lax.axis_index(axis) - len(lower)
+    tiles = tiles[(jnp.arange(peers) - shift) % peers]
+    return joined_along(tiles, dim)
 
 
 def inverse_rms(vector):
@@ -181,9 +203,7 @@
     slot_inputs = jnp.where(filled[:, None], normed_two[owner_rows // TOPK], zero_half).reshape(
         E, CAP, D
     )
-    produced, gate_pre, up_pre = expert_forward(
-        slot_inputs, lax.all_gather(expert_weights, "fsdp", axis=0, tiled=True)
-    )
+    produced, gate_pre, up_pre = expert_forward(slot_inputs, ring_gather(expert_weights, "fsdp", 0))
     picked = produced.reshape(E * CAP, D)[slot_ids].reshape(tokens, TOPK, D)
     mixture = jnp.einsum("tk,tkd->td", gate_probs, picked, preferred_element_type=jnp.float32)
     layer_out = (after + residual_scale * mixture).astype(jnp.bfloat16)

time: 2160 us -> 2740 us (1.27)
  blocking collectives: 59.8 us -> 361 us
  waiting for transfers between devices: 1710 us -> 1830 us
  local copies, waits for them, and re-layouts: 90.1 us -> 209 us
  other arithmetic: 89.7 us -> 125 us
    ppermute x0 -> x7, waiting for transfers between devices: none -> 566 us  [the longest x4 535 us: ring_gather(): lower.append(lax.ppermute(lower[-1] if lower else x, axis, pairs))]
    all_gather x1, waiting for transfers between devices: 416 us -> 0.01 us  [body(): lax.all_gather(expert_weights, 'fsdp', axis=0, tiled=True)]
    all_gather x1, blocking collectives: 13.5 us -> 314 us  [body(): lax.all_gather(norm1_gain, 'fsdp', axis=0, tiled=True)]
    gather x0 -> x5, local copies, waits for them, and re-layouts: none -> 76.7 us  [ring_gather(): tiles = tiles[(jnp.arange(peers) - shift) % peers]]
    unnamed x127 -> x164, local copies, waits for them, and re-layouts: 29 us -> 69.5 us
    reduce_scatter x1, waiting for transfers between devices: 0.02 us -> 34.5 us  [body(): lax.psum_scatter(grad_output_w, 'fsdp', scatter_dimension=0, tiled=True)]
    unnamed x0 -> x3, other arithmetic: none -> 32.7 us
  transfers between devices with their start and end apart: 12 -> 19, of which waited for: 7 -> 8; matrix products, arithmetic and copies ran while one was open for 9% -> 15% of each run, Pallas kernels for 0% -> 0%
where the time goes in v1:
time: 2740 us; the launch traced here: 2730 us
  waiting for transfers between devices  1830 us (67%)
  blocking collectives  361 us (13%)
  local copies, waits for them, and re-layouts  209 us (8%)
  matrix products  181 us (7%)
  other arithmetic  125 us (5%)
    reduce_scatter x1, waiting for transfers between devices, body(): lax.psum_scatter(expert_grads(slot_inputs, slot_grads, gate_pre, up_pre,...  955 us
    ppermute x4, waiting for transfers between devices, ring_gather(): lower.append(lax.ppermute(lower[-1] if lower else x, axis, pairs))  535 us
    all_gather x1, blocking collectives, body(): lax.all_gather(norm1_gain, 'fsdp', axis=0, tiled=True)  314 us
    psum x1, waiting for transfers between devices, body(): lax.psum((shard_gain_one, shard_query, shard_key, shard_value, shard_outp...  258 us
    gather x5, local copies, waits for them, and re-layouts, ring_gather(): tiles = tiles[(jnp.arange(peers) - shift) % peers]  76.7 us
    unnamed x164, local copies, waits for them, and re-layouts  69.5 us
    concatenate x1, other arithmetic, expert_grads(): jnp.concatenate([jnp.einsum('ecf,ecd->efd', grad_gate, slot_inputs, prefe...  66.8 us
  transfers between devices with their start and end apart: 19, of which 8 were waited for; matrix products, arithmetic and copies ran while one was open for 15% of the time, Pallas kernels for 0%

profile of v1, /device:TPU:0, one launch (start us, length us, event | category | flops | bytes accessed | tf_op | source)
XLA Modules:
  0.0 2727.6 jit_solution(15474203655853255074)
XLA Ops:
  11.2 81.3 %collective-permute-done = bf16[2,1536,1024]{2,1,0:T(8,128)(2,1)S(1)} collective-permute-done((bf16[2,1536,1024]{2,1,0:T(8,128)(2,1)}, bf16[2,1536,1024]{2,1,0:T(8,128)(2,1)S(1)}, u32[]{:S(2)}, u32[]{:S(2)}) %collective-permute-start) | collective-permute-done | bytes 6291488 | tf_op jit(solution)/shard_map/ppermute | solution.py:34
  98.8 214.6 %collective-permute-done.1 = bf16[2,1536,1024]{2,1,0:T(8,128)(2,1)} collective-permute-done((bf16[2,1536,1024]{2,1,0:T(8,128)(2,1)S(1)}, bf16[2,1536,1024]{2,1,0:T(8,128)(2,1)}, u32[]{:S(2)}, u32[]{:S(2)}) %collective-permute-start.1) | collective-permute-done | bytes 6291488 | tf_op jit(solution)/shard_map/ppermute | solution.py:34
  331.5 239.2 %collective-permute-done.2 = bf16[2,1536,1024]{2,1,0:T(8,128)(2,1)} collective-permute-done((bf16[2,1536,1024]{2,1,0:T(8,128)(2,1)}, bf16[2,1536,1024]{2,1,0:T(8,128)(2,1)}, u32[]{:S(2)}, u32[]{:S(2)}) %collective-permute-start.2) | collective-permute-done | bytes 6291488 | tf_op jit(solution)/shard_map/ppermute | solution.py:34
  571.2 314.4 %all-gather = bf16[8,1,128]{2,1,0:T(2,128)(2,1)S(1)} all-gather(bf16[1,1,128]{2,1,0:T(2,128)(2,1)S(1)} %bitcast.231), channel_id=1, replica_groups=mesh['replica'=4,'fsdp'=8] {'fsdp'}, dimensions={0}, use_global_device_ids=true | all-gather | bytes 2304 | tf_op jit(solution)/shard_map/all_gather | solution.py:121
  894.6 12.7 all_gather.30
  975.6 30.3 %collective-permute-done.6 = bf16[2,1536,1024]{2,1,0:T(8,128)(2,1)S(1)} collective-permute-done((bf16[2,1536,1024]{2,1,0:T(8,128)(2,1)}, bf16[2,1536,1024]{2,1,0:T(8,128)(2,1)S(1)}, u32[]{:S(2)}, u32[]{:S(2)}) %collective-permute-start.6) | collective-permute-done | bytes 6291488 | tf_op jit(solution)/shard_map/ppermute | solution.py:36
  1009.4 32.9 %fusion.111 = (bf16[8,2,384,1024]{3,2,1,0:T(8,128)(2,1)}, bf16[8,2,384,1024]{3,2,1,0:T(8,128)(2,1)}, bf16[8,2,384,1024]{3,2,1,0:T(8,128)(2,1)}, bf16[8,2,384,1024]{3,2,1,0:T(8,128)(2,1)}) fusion(bf16[8,2,1536,1024]{3,2,1,0:T(8,128)(2,1)} %bitcast_dynamic-update-slice_fusion), kind=kLoop, calls=%fused_computation.205 | loop fusion | bytes 100663296 | tf_op jit(solution)/shard_map/gather | solution.py:39
  1086.1 32.7 %pad_maximum_fusion.1 = bf16[8,2,1536,1024]{3,2,1,0:T(8,128)(2,1)} fusion(bf16[8,2,384,1024]{3,2,1,0:T(8,128)(2,1)} %gather_fusion.7, bf16[8,2,384,1024]{3,2,1,0:T(8,128)(2,1)} %gather_fusion.6, bf16[8,2,384,1024]{3,2,1,0:T(8,128)(2,1)} %gather_fusion.5, bf16[8,2,384,1024]{3,2,1,0:T(8,128)(2,1)} %gather_fusion.4), kind=kLoop, calls=%fused_computation.10 | loop fusion | flops 201326592 | bytes 100663296
  1130.3 13.4 multiply_convert_fusion.2
  1155.3 14.0 gather_fusion.1
  1176.8 13.8 gather_fusion.2
  1195.0 14.4 multiply_convert_fusion.1
  1209.4 12.4 fusion
  1221.8 12.1 add_convert_fusion
  1234.0 13.9 gather_fusion.3
  1279.8 19.2 fusion.21
  1303.0 18.5 fusion.24
  1321.5 19.1 fusion.25
  1340.6 66.8 %pad_maximum_fusion = f32[16,1536,1024]{2,1,0:T(8,128)} fusion(f32[16,512,1024]{2,1,0:T(8,128)} %fusion.21, f32[16,512,1024]{2,1,0:T(8,128)} %fusion.24, f32[16,512,1024]{2,1,0:T(8,128)} %fusion.25), kind=kLoop, calls=%fused_computation.9 | loop fusion | flops 50331648 | bytes 201326592 | tf_op jit(solution)/shard_map/concatenate | solution.py:96
  1409.4 34.5 %reduce-scatter.13.cloned.1.call-done = f32[128,1024]{1,0:T(8,128)} async-done(((f32[1024,1024]{1,0:T(8,128)}), f32[128,1024]{1,0:T(8,128)}) %reduce-scatter.13.cloned.1.call-update) | async-done | bytes 524304 | tf_op jit(solution)/shard_map/reduce_scatter | solution.py:310
  1443.9 955.4 %reduce-scatter.17.cloned.1.call-done = f32[2,1536,1024]{2,1,0:T(8,128)} async-done(((f32[16,1536,1024]{2,1,0:T(8,128)}), f32[2,1536,1024]{2,1,0:T(8,128)}) %reduce-scatter.17.cloned.1.call-update) | async-done | bytes 12582928 | tf_op jit(solution)/shard_map/reduce_scatter | solution.py:229
  2407.4 13.9 all-reduce.2
  2443.0 258.2 %all-reduce.7.cloned.1.call-done = (f32[128,1024]{1,0:T(8,128)}, f32[128,512]{1,0:T(8,128)}, f32[128,512]{1,0:T(8,128)}, f32[128,1024]{1,0:T(8,128)}, f32[2,1536,1024]{2,1,0:T(8,128)}) async-done(((f32[128,1024]{1,0:T(8,128)}, f32[128,512]{1,0:T(8,128)}, f32[128,512]{1,0:T(8,128)}, f32[128,1024]{1,0:T(8,128)}, f32[2,1536,1024]{2,1,0:T(8,128)}), (f32[128,1024]{1,0:T(8,128)}, f32[128,512]{1,0:T(8,128)}, ...) | async-done | bytes 14155792 | tf_op jit(solution)/shard_map/psum | solution.py:314
  2708.3 12.1 copy.114
  (307 shorter events, 261.4 us)
Async XLA Ops:
  7.2 564.0 %copy-start.66 = (bf16[128]{0:T(256)(128)(2,1)S(1)}, bf16[128]{0:T(256)(128)(2,1)}, u32[]{:S(2)}) copy-start(bf16[128]{0:T(256)(128)(2,1)} %param.15) | copy-start | bytes 772
  7.2 878.5 %copy-start.67 = (bf16[128]{0:T(256)(128)(2,1)S(1)}, bf16[128]{0:T(256)(128)(2,1)}, u32[]{:S(2)}) copy-start(bf16[128]{0:T(256)(128)(2,1)} %param.20) | copy-start | bytes 772
  7.2 887.3 %copy-start.65 = (bf16[128,16]{0,1:T(8,128)(2,1)S(1)}, bf16[128,16]{0,1:T(8,128)(2,1)}, u32[]{:S(2)}) copy-start(bf16[128,16]{0,1:T(8,128)(2,1)} %param.21) | copy-start | bytes 12292
  7.2 901.4 %copy-start.4 = (bf16[256,1024]{1,0:T(8,128)(2,1)S(1)}, bf16[256,1024]{1,0:T(8,128)(2,1)}, u32[]{:S(2)}) copy-start(bf16[256,1024]{1,0:T(8,128)(2,1)} %param.12) | copy-start | bytes 1572868
  7.2 905.0 %all-gather.8.cloned.1.call-start = ((), (), s32[]{:S(2)}) async-start(), calls=%async_computation.6 | async-start | bytes 1179648 | tf_op jit(solution)/shard_map/all_gather | solution.py:124
  8.0 906.1 %all-gather.10.cloned.1.call-start = ((), (), s32[]{:S(2)}) async-start(), calls=%async_computation.7 | async-start | bytes 1179648 | tf_op jit(solution)/shard_map/all_gather | solution.py:123
  8.7 907.5 %all-gather.12.cloned.1.call-start = ((), (), s32[]{:S(2)}) async-start(), calls=%async_computation.8 | async-start | bytes 2359296 | tf_op jit(solution)/shard_map/all_gather | solution.py:122
  9.5 900.7 %copy-start.16 = (bf16[256,1024]{1,0:T(8,128)(2,1)S(1)}, bf16[256,1024]{1,0:T(8,128)(2,1)}, u32[]{:S(2)}) copy-start(bf16[256,1024]{1,0:T(8,128)(2,1)} %param.23) | copy-start | bytes 1572868
  9.5 914.2 %all-gather.14.cloned.1.call-start = ((), (), s32[]{:S(2)}) async-start(), calls=%async_computation.9 | async-start | bytes 2359296 | tf_op jit(solution)/shard_map/all_gather | solution.py:125
  10.0 1185.0 %all-gather.16.cloned.1.call-start = ((), (), s32[]{:S(2)}) async-start(), calls=%async_computation.10 | async-start | bytes 56623104 | tf_op jit(solution)/shard_map/all_gather | solution.py:227
  10.6 1398.7 %reduce-scatter.9.cloned.1.call-start = ((), (), s32[]{:S(2)}) async-start(), calls=%async_computation.12 | async-start | bytes 2359296 | tf_op jit(solution)/shard_map/reduce_scatter | solution.py:308
  10.7 81.8 %collective-permute-start = (bf16[2,1536,1024]{2,1,0:T(8,128)(2,1)}, bf16[2,1536,1024]{2,1,0:T(8,128)(2,1)S(1)}, u32[]{:S(2)}, u32[]{:S(2)}) collective-permute-start(bf16[2,1536,1024]{2,1,0:T(8,128)(2,1)} %param.22), channel_id=1, source_target_pairs={{0,1},{1,2},{2,3},{3,4},{4,5},{5,6},{6,7},{7,0},{8,9},{9,10},{10,1... | collective-permute-start | bytes 18874376 | tf_op jit(solution)/shard_map/ppermute | solution.py:34
  95.2 218.2 %collective-permute-start.1 = (bf16[2,1536,1024]{2,1,0:T(8,128)(2,1)S(1)}, bf16[2,1536,1024]{2,1,0:T(8,128)(2,1)}, u32[]{:S(2)}, u32[]{:S(2)}) collective-permute-start(bf16[2,1536,1024]{2,1,0:T(8,128)(2,1)S(1)} %collective-permute-done), channel_id=1, source_target_pairs={{0,1},{1,2},{2,3},{3,4},{4,5},{5,6},{6,7},{7,0},{8,9},{9,10},{10,1... | collective-permute-start | bytes 18874376 | tf_op jit(solution)/shard_map/ppermute | solution.py:34
  95.2 232.6 %collective-permute-start.4 = (bf16[2,1536,1024]{2,1,0:T(8,128)(2,1)}, bf16[2,1536,1024]{2,1,0:T(8,128)(2,1)}, u32[]{:S(2)}, u32[]{:S(2)}) collective-permute-start(bf16[2,1536,1024]{2,1,0:T(8,128)(2,1)} %param.22), channel_id=1, source_target_pairs={{1,0},{2,1},{3,2},{4,3},{5,4},{6,5},{7,6},{0,7},{9,8},{10,9},{11,1... | collective-permute-start | bytes 18874376 | tf_op jit(solution)/shard_map/ppermute | solution.py:36
  313.4 257.3 %collective-permute-start.2 = (bf16[2,1536,1024]{2,1,0:T(8,128)(2,1)}, bf16[2,1536,1024]{2,1,0:T(8,128)(2,1)}, u32[]{:S(2)}, u32[]{:S(2)}) collective-permute-start(bf16[2,1536,1024]{2,1,0:T(8,128)(2,1)} %collective-permute-done.1), channel_id=1, source_target_pairs={{0,1},{1,2},{2,3},{3,4},{4,5},{5,6},{6,7},{7,0},{8,9},{9,10},{10,1... | collective-permute-start | bytes 18874376 | tf_op jit(solution)/shard_map/ppermute | solution.py:34
  327.9 608.6 %collective-permute-start.5 = (bf16[2,1536,1024]{2,1,0:T(8,128)(2,1)}, bf16[2,1536,1024]{2,1,0:T(8,128)(2,1)}, u32[]{:S(2)}, u32[]{:S(2)}) collective-permute-start(bf16[2,1536,1024]{2,1,0:T(8,128)(2,1)} %collective-permute-done.4), channel_id=1, source_target_pairs={{1,0},{2,1},{3,2},{4,3},{5,4},{6,5},{7,6},{0,7},{9,8},{10,9},{11,1... | collective-permute-start | bytes 18874376 | tf_op jit(solution)/shard_map/ppermute | solution.py:36
  570.7 367.1 %collective-permute-start.3 = (bf16[2,1536,1024]{2,1,0:T(8,128)(2,1)}, bf16[2,1536,1024]{2,1,0:T(8,128)(2,1)}, u32[]{:S(2)}, u32[]{:S(2)}) collective-permute-start(bf16[2,1536,1024]{2,1,0:T(8,128)(2,1)} %collective-permute-done.2), channel_id=1, source_target_pairs={{0,1},{1,2},{2,3},{3,4},{4,5},{5,6},{6,7},{7,0},{8,9},{9,10},{10,1... | collective-permute-start | bytes 18874376 | tf_op jit(solution)/shard_map/ppermute | solution.py:34
  936.4 69.5 %collective-permute-start.6 = (bf16[2,1536,1024]{2,1,0:T(8,128)(2,1)}, bf16[2,1536,1024]{2,1,0:T(8,128)(2,1)S(1)}, u32[]{:S(2)}, u32[]{:S(2)}) collective-permute-start(bf16[2,1536,1024]{2,1,0:T(8,128)(2,1)} %collective-permute-done.5), channel_id=1, source_target_pairs={{1,0},{2,1},{3,2},{4,3},{5,4},{6,5},{7,6},{0,7},{9,8},{10,9},{11,1... | collective-permute-start | bytes 18874376 | tf_op jit(solution)/shard_map/ppermute | solution.py:36
  1267.6 141.7 %reduce-scatter.11.cloned.1.call-start = ((), (), s32[]{:S(2)}) async-start(), calls=%async_computation.13 | async-start | bytes 2359296 | tf_op jit(solution)/shard_map/reduce_scatter | solution.py:309
  1273.3 136.1 %reduce-scatter.7.cloned.1.call-start = ((), (), s32[]{:S(2)}) async-start(), calls=%async_computation.11 | async-start | bytes 4718592 | tf_op jit(solution)/shard_map/reduce_scatter | solution.py:307
  1279.5 164.4 %reduce-scatter.13.cloned.1.call-start = ((), (), s32[]{:S(2)}) async-start(), calls=%async_computation.14 | async-start | bytes 4718592 | tf_op jit(solution)/shard_map/reduce_scatter | solution.py:310
  1302.9 1096.4 %reduce-scatter.17.cloned.1.call-start = ((), (), s32[]{:S(2)}) async-start(), calls=%async_computation.16 | async-start | bytes 113246208 | tf_op jit(solution)/shard_map/reduce_scatter | solution.py:229
  1407.4 1023.2 %reduce-scatter.15.cloned.1.call-start = ((), (), s32[]{:S(2)}) async-start(), calls=%async_computation.15 | async-start | bytes 73728 | tf_op jit(solution)/shard_map/reduce_scatter | solution.py:312
  1409.3 1291.9 %all-reduce.7.cloned.1.call-start = ((), (), s32[]{:S(2)}) async-start(), calls=%async_computation.17 | async-start | bytes 28311552 | tf_op jit(solution)/shard_map/psum | solution.py:314
  (69 other events, 1176.8 us)
Sparse Core Ops, SparseCore 0:
  9.7 84.3 all-gather.7
  95.7 26.3 all-gather.9
  123.7 42.9 all-gather.11
  168.1 45.5 all-gather.13
  215.2 671.0 all-gather.15
  1267.8 37.0 reduce-scatter.8
  1307.1 34.5 reduce-scatter.10
  1344.6 48.7 reduce-scatter.6
  1395.7 48.1 reduce-scatter.12
  1446.1 953.1 reduce-scatter.16
  2402.2 28.3 reduce-scatter.14
  2434.9 266.2 all-reduce.6
